TPU v7x, 512 devices: a whole 4x8x8 slice. The times are simulated.
512 devices in a mesh: lang: 16 (over z_lo, y), bulk: 32 (over z_hi, x, core).
Axes of the slice: x: 4, y: 8, z: 8 (z_hi: 4, z_lo: 2; z = z_hi * 2 + z_lo), core: 2. Of those that a mesh axis runs over, the one named last changes fastest.
Arguments:
- sources: bfloat16 [524288, 1024], P(('lang', 'bulk')), may hold values from -24 to 24
- lang_ids: int32 [4096], P(('lang', 'bulk')), may hold values from 0 to 15
- centers: float32 [16, 1024], replicated, may hold values from -3 to 3
- targets: bfloat16 [1024, 1024], P('bulk'), may hold values from -12 to 12
Outputs:
- hubness: float32 [1024], P('bulk')
- source_logsum: float32 [524288], P(('lang', 'bulk'))
- source_match: float32 [524288], P(('lang', 'bulk'))
All inputs are finite; a program needn't handle non-finite values.
Results may differ from a plain program's by a relative error of at most 0.0043.
Values may be sent and summed in bfloat16 or wider, within the bound.
A program may use at most 64 MiB of HBM per device.

v0:
```python
import jax
import jax.numpy as jnp
from jax import lax
from jax.sharding import PartitionSpec as P


def tile_scores(target_piece, centered, temper):
    products = lax.dot_general(
        target_piece, centered, (((1,), (1,)), ((), ())), preferred_element_type=jnp.float32
    )
    return products * temper


def read_update(carried, score_tile, hub_part):
    run_peak, run_weight, run_match = carried
    adjusted = 2.0 * score_tile - hub_part[:, None]
    new_peak = jnp.max(adjusted, axis=0)
    weights = jnp.exp(adjusted - new_peak[None, :])
    factor = jnp.exp(run_peak - new_peak)
    return (
        new_peak,
        run_weight * factor + jnp.sum(weights, axis=0),
        run_match * factor + jnp.sum(weights * score_tile, axis=0),
    )


def per_device(sources, lang_ids, centers, targets):
    source_count, feature_width = sources.shape
    block_count = lang_ids.shape[0]
    lang_count = centers.shape[0]
    temper = feature_width ** (-0.5)
    target_local = targets.shape[0]
    chosen = (lang_ids[:, None] == jnp.arange(lang_count, dtype=jnp.int32)[None, :]).astype(
        jnp.float32
    )
    offsets = jnp.dot(
        chosen, centers, precision=lax.Precision.HIGHEST, preferred_element_type=jnp.float32
    )
    grouped = sources.astype(jnp.float32).reshape(
        block_count, source_count // block_count, feature_width
    )
    centered = (
        (grouped - offsets[:, None, :]).reshape(source_count, feature_width).astype(jnp.bfloat16)
    )
    score_tile = tile_scores(lax.all_gather(targets, "bulk", axis=0, tiled=True), centered, temper)
    tile_peak = jnp.max(score_tile, axis=1)
    tile_weight = jnp.sum(jnp.exp(score_tile - tile_peak[:, None]), axis=1)
    score_tile, tile_peak, tile_weight = (score_tile, tile_peak, tile_weight)
    global_peak = lax.pmax(tile_peak, ("lang", "bulk"))
    global_weight = lax.psum(tile_weight * jnp.exp(tile_peak - global_peak), ("lang", "bulk"))
    hubness = global_peak + jnp.log(global_weight)
    start_state = (
        jnp.full((source_count,), -jnp.inf, jnp.float32),
        jnp.zeros((source_count,), jnp.float32),
        jnp.zeros((source_count,), jnp.float32),
    )
    score_tile = tile_scores(lax.all_gather(targets, "bulk", axis=0, tiled=True), centered, temper)
    final_state = read_update(start_state, score_tile, hubness)
    source_logsum = final_state[0] + jnp.log(final_state[1])
    source_match = final_state[2] / final_state[1]
    own_hub = lax.dynamic_slice_in_dim(hubness, lax.axis_index("bulk") * target_local, target_local)
    return (own_hub, source_logsum, source_match)


def solution(mesh):
    in_specs = (P(("lang", "bulk"), None), P(("lang", "bulk")), P(), P("bulk", None))
    out_specs = (P("bulk"), P(("lang", "bulk")), P(("lang", "bulk")))
    return jax.shard_map(
        per_device, mesh=mesh, in_specs=in_specs, out_specs=out_specs, check_vma=False
    )
```

profile of v0, /device:TPU:1, one launch (start us, length us, event | category | flops | bytes accessed | tf_op | source)
XLA Modules:
  0.0 289.6 jit_solution(16624731422087546585)
XLA Ops:
  7.2 0.0 copy-start
  7.2 0.0 all-gather.2.cloned.1.call-start
  7.2 0.7 all-gather.2.cloned.1.call-update
  7.9 0.1 copy-done
  8.0 0.9 fusion.3
  8.9 2.1 fusion
  11.0 66.6 %all-gather.2.cloned.1.call-done = bf16[1024,1024]{1,0:T(8,128)(2,1)} async-done(((bf16[32,1024]{1,0:T(8,128)(2,1)}), bf16[1024,1024]{1,0:T(8,128)(2,1)}) %all-gather.2.cloned.1.call-update) | async-done | bytes 2097168 | tf_op jit(solution)/shard_map/all_gather | solution.py:45
  77.6 5.9 %multiply_reduce_fusion.1 = (f32[1024]{0:T(1024)S(1)}, f32[1024,1024]{0,1:T(8,128)}) fusion(bf16[1024,1024]{1,0:T(8,128)(2,1)S(1)} %fusion, bf16[1024,1024]{1,0:T(8,128)(2,1)} %all-gather.2.cloned.1.call-done), kind=kOutput, calls=%fused_computation.7 | convolution fusion | flops 2149579776 | bytes 8392704 | tf_op jit(solution)/shard_map/dot_general | solution.py:8
  83.5 95.8 %pmax.7 = f32[1024]{0:T(1024)S(1)} all-reduce(f32[1024]{0:T(1024)S(1)} %get-tuple-element.7), channel_id=1, replica_groups=mesh['lang'=16,'bulk'=32] {'lang','bulk'}, use_global_device_ids=true, to_apply=%region_1.0 | all-reduce | flops 1024 | bytes 8192 | tf_op jit(solution)/shard_map/pmax | solution.py:49
  179.3 3.1 %exponential_reduce_fusion = f32[1024]{0:T(1024)S(1)} fusion(f32[1024,1024]{0,1:T(8,128)} %get-tuple-element.8, f32[1024]{0:T(1024)S(1)} %get-tuple-element.7), kind=kLoop, calls=%fused_computation.2 | loop fusion | flops 3144704 | bytes 4202496 | tf_op jit(solution)/shard_map/reduce_sum | solution.py:47
  182.4 94.4 %psum.7 = f32[1024]{0:T(1024)S(1)} all-reduce(f32[1024]{0:T(1024)S(1)} %exponential_multiply_fusion.1), channel_id=1, replica_groups=mesh['lang'=16,'bulk'=32] {'lang','bulk'}, use_global_device_ids=true, to_apply=%region_3.0 | all-reduce | flops 1024 | bytes 8192 | tf_op jit(solution)/shard_map/psum | solution.py:50
  276.8 0.0 copy-start.1
  276.8 2.8 fusion.1
  279.6 0.6 copy-done.1
  280.2 1.3 multiply_reduce_fusion
  281.5 0.6 dynamic_slice.3
  282.1 0.6 add_divide_fusion
  (2 shorter events, 0.0 us)
Async XLA Ops:
  7.2 0.8 copy-start
  7.2 70.4 %all-gather.2.cloned.1.call-start = ((), (), s32[]{:S(2)}) async-start(), calls=%async_computation | async-start | bytes 2162688 | tf_op jit(solution)/shard_map/all_gather | solution.py:45
  276.8 3.4 %copy-start.1 = (f32[1024,1024]{0,1:T(8,128)S(1)}, f32[1024,1024]{0,1:T(8,128)}, u32[]{:S(2)}) copy-start(f32[1024,1024]{0,1:T(8,128)} %get-tuple-element.8) | copy-start | bytes 12582916
Sparse Core Ops, SparseCore 0:
  11.1 66.4 all-gather.1
where the time goes:
time: 290 us
  blocking collectives  190 us (66%)
  waiting for transfers between devices  67.3 us (23%)
  between operations  14.1 us (5%)
  other arithmetic  9.93 us (3%)
  matrix products  6.74 us (2%)
    pmax x1, blocking collectives, per_device(): global_peak = lax.pmax(tile_peak, ('lang', 'bulk'))  95.8 us
    psum x1, blocking collectives, per_device(): lax.psum(tile_weight * jnp.exp(tile_peak - global_peak), ('lang', 'bulk'))  94.4 us
    all_gather x1, waiting for transfers between devices, per_device(): lax.all_gather(targets, 'bulk', axis=0, tiled=True)  66.6 us
    dot_general x1, matrix products, tile_scores(): lax.dot_general(target_piece, centered, (((1,), (1,)), ((), ())), preferr...  5.89 us
  transfers between devices with their start and end apart: 1, of which 1 were waited for; matrix products, arithmetic and copies ran while one was open for 1% of the time, Pallas kernels for 0%

commit v1 on v0

--- a/solution.py
+++ b/solution.py
@@ -47,7 +47,9 @@
     tile_weight = jnp.sum(jnp.exp(score_tile - tile_peak[:, None]), axis=1)
     score_tile, tile_peak, tile_weight = (score_tile, tile_peak, tile_weight)
     global_peak = lax.pmax(tile_peak, ("lang", "bulk"))
-    global_weight = lax.psum(tile_weight * jnp.exp(tile_peak - global_peak), ("lang", "bulk"))
+    block = tile_weight * jnp.exp(tile_peak - global_peak)
+    blocks = lax.all_gather(block, ("lang", "bulk"))
+    global_weight = jnp.sum(blocks, axis=0)
     hubness = global_peak + jnp.log(global_weight)
     start_state = (
         jnp.full((source_count,), -jnp.inf, jnp.float32),

time: 290 us -> 960 us (3.31)
  waiting for transfers between devices: 67.3 us -> 829 us
  blocking collectives: 190 us -> 95.8 us
    all_gather x0 -> x1, waiting for transfers between devices: none -> 762 us  [per_device(): blocks = lax.all_gather(block, ('lang', 'bulk'))]
    psum x1 -> x0, blocking collectives: 94.4 us -> none  [per_device(): lax.psum(tile_weight * jnp.exp(tile_peak - global_peak), ('lang', 'bulk'))]
  transfers between devices with their start and end apart: 1 -> 2, of which waited for: 1 -> 2; matrix products, arithmetic and copies ran while one was open for 1% -> 0% of each run, Pallas kernels for 0% -> 0%
where the time goes in v1:
time: 960 us
  waiting for transfers between devices  829 us (86%)
  blocking collectives  95.8 us (10%)
  between operations  14.1 us (1%)
  other arithmetic  10.7 us (1%)
    all_gather x1, waiting for transfers between devices, per_device(): blocks = lax.all_gather(block, ('lang', 'bulk'))  762 us
    pmax x1, blocking collectives, per_device(): global_peak = lax.pmax(tile_peak, ('lang', 'bulk'))  95.8 us
    all_gather x1, waiting for transfers between devices, per_device(): lax.all_gather(targets, 'bulk', axis=0, tiled=True)  66.6 us
  transfers between devices with their start and end apart: 2, of which 2 were waited for; matrix products, arithmetic and copies ran while one was open for 0% of the time, Pallas kernels for 0%

profile of v1, /device:TPU:1, one launch (start us, length us, event | category | flops | bytes accessed | tf_op | source)
XLA Modules:
  0.0 959.8 jit_solution(7335659766481432970)
XLA Ops:
  7.2 0.0 copy-start
  7.2 0.0 all-gather.4.cloned.1.call-start
  7.2 0.7 all-gather.4.cloned.1.call-update
  7.9 0.0 all-gather.6.cloned.1.call-start
  8.0 0.0 copy-done
  8.0 0.9 fusion.3
  8.9 2.1 fusion
  11.0 66.6 %all-gather.4.cloned.1.call-done = bf16[1024,1024]{1,0:T(8,128)(2,1)} async-done(((bf16[32,1024]{1,0:T(8,128)(2,1)}), bf16[1024,1024]{1,0:T(8,128)(2,1)}) %all-gather.4.cloned.1.call-update) | async-done | bytes 2097168 | tf_op jit(solution)/shard_map/all_gather | solution.py:45
  77.6 5.9 multiply_reduce_fusion.1
  83.5 95.8 %pmax.7 = f32[1024]{0:T(1024)S(1)} all-reduce(f32[1024]{0:T(1024)S(1)} %get-tuple-element.7), channel_id=1, replica_groups=mesh['lang'=16,'bulk'=32] {'lang','bulk'}, use_global_device_ids=true, to_apply=%region_1.0 | all-reduce | flops 1024 | bytes 8192 | tf_op jit(solution)/shard_map/pmax | solution.py:49
  179.3 3.1 exponential_reduce_fusion
  182.4 0.6 exponential_multiply_fusion.1
  183.0 0.0 all-gather.6.cloned.1.call-update
  183.0 762.1 %all-gather.6.cloned.1.call-done = f32[524288]{0:T(1024)} async-done(((f32[1024]{0:T(1024)}), f32[524288]{0:T(1024)}) %all-gather.6.cloned.1.call-update) | async-done | bytes 2097168 | tf_op jit(solution)/shard_map/all_gather | solution.py:51
  945.1 1.7 reshape.14
  946.8 0.1 reduce_sum.37
  947.0 0.0 copy-start.1
  947.0 2.8 fusion.1
  949.8 0.6 copy-done.1
  950.4 1.3 multiply_reduce_fusion
  951.7 0.6 dynamic_slice.3
  952.3 0.6 add_divide_fusion
  (1 shorter events, 0.0 us)
Async XLA Ops:
  7.2 0.8 copy-start
  7.2 70.4 %all-gather.4.cloned.1.call-start = ((), (), s32[]{:S(2)}) async-start(), calls=%async_computation | async-start | bytes 2162688 | tf_op jit(solution)/shard_map/all_gather | solution.py:45
  7.9 937.2 %all-gather.6.cloned.1.call-start = ((), (), s32[]{:S(2)}) async-start(), calls=%async_computation.1 | async-start | bytes 2101248 | tf_op jit(solution)/shard_map/all_gather | solution.py:51
  947.0 3.4 copy-start.1
Sparse Core Ops, SparseCore 0:
  11.1 66.4 all-gather.3
  183.1 761.9 all-gather.5
